TPU v7x, 512 devices: a whole 4x4x16 slice. The times are simulated.
512 devices in a mesh: tp: 16 (over z_lo, core), lat: 32 (over y, x, z_hi).
Axes of the slice: x: 4, y: 4, z: 16 (z_hi: 2, z_lo: 8; z = z_hi * 8 + z_lo), core: 2. Of those that a mesh axis runs over, the one named last changes fastest.
Arguments:
- resid: bfloat16 [256, 8192], P(None, 'tp'), may hold values from -6 to 6
- gain: float32 [8192], P('tp'), may hold values from 0.2 to 2.5
- w_gate: bfloat16 [8192, 28672], P('tp', 'lat'), may hold values from -0.0625 to 0.0625
- w_up: bfloat16 [8192, 28672], P('tp', 'lat'), may hold values from -0.0625 to 0.0625
- w_down: bfloat16 [28672, 8192], P('lat', 'tp'), may hold values from -0.0625 to 0.0625
- cotangent: bfloat16 [256, 8192], P(None, 'tp'), may hold values from -6 to 6
- enc_tiles: bfloat16 [160, 8192, 128], P('lat', 'tp'), may hold values from -0.0625 to 0.0625
- enc_bias: float32 [160, 128], P('lat'), may hold values from -3 to 3
- dec_tiles: bfloat16 [160, 128, 8192], P('lat', None, 'tp'), may hold values from -0.0625 to 0.0625
- tile_blocks: int32 [160], P('lat'), may hold values from 0 to 8192, as said below
- owner_counts: int32 [32], P('lat'), may hold values from 1 to 5, as said below
- token_blocks: int32 [256, 64], replicated, may hold values from 0 to 8192, as said below
Outputs:
- resid_grad: bfloat16 [256, 8192], P(None, 'tp')
- attribution: float32 [256, 160, 128], P('tp', 'lat')
Inputs may be any that keep to these rules, and one draw needn't show every extreme that they name: `tile_blocks`: owner o holds tile slots o * 5 to o * 5 + 4; its first owner_counts[o] slots hold distinct block ids below 8192, the other slots hold 8192. `owner_counts`: some owner uses all 5 slots. `token_blocks`: 8192 marks an empty slot; an id may stand more than once in one token's list.
All inputs are finite; a program needn't handle non-finite values.
Results may differ from a plain program's by a relative error of at most 0.0054.
Values may be sent and summed in bfloat16 or wider, within the bound.
A program may use at most 64 MiB of HBM per device.

v0:
```python
import jax
import jax.numpy as jnp
from jax import lax
from jax.sharding import PartitionSpec as P


def copy_for_each(x, axis):
    devices = lax.axis_size(axis)
    return lax.all_to_all(jnp.broadcast_to(x[None], (devices, *x.shape)), axis, 0, 0, tiled=True)


def of_everyone(x, axis):
    return copy_for_each(x, axis).sum(axis=0)


def in_one_piece(arrays, axis, dim, along):
    ends, at = ([], 0)
    for a in arrays[:-1]:
        at += a.shape[along]
        ends.append(at)
    both = jnp.concatenate(arrays, axis=along)
    return tuple(
        jnp.split(lax.psum_scatter(both, axis, scatter_dimension=dim, tiled=True), ends, axis=along)
    )


def in_one_piece_2(arrays, axis, dim, along):
    widths = [a.shape[along] for a in arrays]
    both = jnp.concatenate(arrays, axis=along)
    result = lax.all_gather(both, axis, axis=dim, tiled=True)
    return tuple(jnp.split(result, [sum(widths[:k]) for k in range(1, len(widths))], axis=along))


def in_blocks(x, dim, devices):
    before, after = (x.shape[:dim], x.shape[dim + 1 :])
    return jnp.moveaxis(x.reshape(*before, devices, -1, *after), dim, 0)


def sum_at_owner(x, axis, dim):
    devices = lax.axis_size(axis)
    pieces = lax.all_to_all(in_blocks(x, dim, devices), axis, 0, 0, tiled=True)
    return jnp.sum(pieces, axis=0)


def filled_up(lines, devices):
    spare = -lines.shape[0] % devices
    if not spare:
        return lines
    return jnp.concatenate([lines, jnp.zeros((spare, *lines.shape[1:]), lines.dtype)])


def laid_out(pieces, dim):
    shape = list(pieces.shape[1:])
    shape[dim] *= pieces.shape[0]
    return jnp.moveaxis(pieces, 0, dim).reshape(shape)


def gathered_copies(x, axis, dim):
    pieces = copy_for_each(x, axis)
    return laid_out(pieces, dim)


def total_of(x, axes):
    lines = x.reshape(-1, x.shape[-1])
    own = sum_at_owner(filled_up(lines, lax.axis_size(axes)), axes, 0)
    whole = gathered_copies(own, axes, 0)
    return whole[: len(lines)].reshape(x.shape)


def hidden_grads(gate, up, hgrad):
    sig = jax.nn.sigmoid(gate)
    d_gate = (hgrad * up * sig * (1.0 + gate * (1.0 - sig))).astype(jnp.bfloat16)
    d_up = (hgrad * gate * sig).astype(jnp.bfloat16)
    return (d_gate, d_up)


def right_product(left, weight):
    return lax.dot_general(
        left, weight, (((1,), (1,)), ((), ())), preferred_element_type=jnp.float32
    )


def on_device(
    resid,
    gain,
    w_gate,
    w_up,
    w_down,
    cotangent,
    enc_tiles,
    enc_bias,
    dec_tiles,
    tile_blocks,
    owner_counts,
    token_blocks,
):
    width = lax.axis_size("tp") * resid.shape[1]
    resid_f = resid.astype(jnp.float32)
    scaled = (resid_f * gain).astype(jnp.bfloat16)
    gate_part = jnp.dot(scaled, w_gate, preferred_element_type=jnp.float32)
    up_part = jnp.dot(scaled, w_up, preferred_element_type=jnp.float32)
    hgrad_part = right_product(cotangent, w_down)
    square_part = jnp.sum(resid_f * resid_f, axis=1)
    squares = of_everyone(square_part, "tp")
    rinv = lax.rsqrt(squares / width + 1e-05)
    gate_own, up_own, hgrad_own = in_one_piece((gate_part, up_part, hgrad_part), "tp", 0, 1)
    share = gate_own.shape[0]
    rinv_own = lax.dynamic_slice_in_dim(rinv, lax.axis_index("tp") * share, share)
    grad_gate, grad_up = hidden_grads(
        rinv_own[:, None] * gate_own, rinv_own[:, None] * up_own, hgrad_own
    )
    d_gate, d_up = in_one_piece_2((grad_gate, grad_up), "tp", 0, 1)
    feat_part = right_product(d_gate, w_gate) + right_product(d_up, w_up)
    feat = total_of(feat_part, "lat")
    norm_term = of_everyone(jnp.sum(resid_f * gain * feat, axis=1), "tp")
    resid_grad = (
        cotangent.astype(jnp.float32)
        + rinv[:, None] * gain * feat
        - resid_f * (rinv**3 * norm_term / width)[:, None]
    ).astype(jnp.bfloat16)
    slots = enc_tiles.shape[0]
    used_count = owner_counts[0]
    rows = resid.shape[0] // lax.axis_size("tp")
    pre = jnp.einsum("td,jdl->tjl", resid, enc_tiles, preferred_element_type=jnp.float32)
    grad = jnp.einsum("td,jld->tjl", resid_grad, dec_tiles, preferred_element_type=jnp.float32)
    terms = sum_at_owner(jnp.stack((pre, grad), axis=2), "tp", 0)
    pre = terms[:, :, 0]
    grad = terms[:, :, 1]
    own_blocks = lax.dynamic_slice_in_dim(token_blocks, lax.axis_index("tp") * rows, rows, 0)
    match = jnp.any(own_blocks[:, :, None] == tile_blocks[None, None, :], axis=1)
    used = jnp.arange(slots, dtype=jnp.int32) < used_count
    live = jnp.logical_and(match, used[None, :]).astype(jnp.float32)
    attribution = -jnp.maximum(pre + enc_bias[None], 0.0) * live[:, :, None] * grad
    return (resid_grad, attribution)


def solution(mesh):
    placed = (
        P(None, "tp"),
        P("tp"),
        P("tp", "lat"),
        P("tp", "lat"),
        P("lat", "tp"),
        P(None, "tp"),
        P("lat", "tp", None),
        P("lat", None),
        P("lat", None, "tp"),
        P("lat"),
        P("lat"),
        P(),
    )
    return jax.shard_map(
        on_device,
        mesh=mesh,
        in_specs=placed,
        out_specs=(P(None, "tp"), P("tp", "lat", None)),
        check_vma=False,
    )
```

profile of v0, /device:TPU:65, one launch (start us, length us, event | category | flops | bytes accessed | tf_op | source)
XLA Modules:
  0.0 321.1 jit_solution(490052936402133853)
XLA Ops:
  7.2 0.0 copy-start
  7.2 0.0 copy-start.4
  7.2 0.0 reduce-scatter.2.cloned.1.call-start
  7.2 1.8 fusion.15
  9.1 1.4 fusion.17
  10.5 0.5 fusion.30
  11.0 1.7 pad_maximum_fusion
  12.7 0.0 reduce-scatter.2.cloned.1.call-update
  12.8 0.9 copy-done.1
  13.7 0.1 fusion.4
  13.8 0.6 broadcast_in_dim.6
  14.4 12.5 %all-to-all-start = ((f32[16,1,256]{2,1,0:T(1,128)}), f32[16,1,256]{2,1,0:T(1,128)S(1)}, u32[]{:S(2)}, u32[]{:S(2)}) async-start(f32[16,1,256]{2,1,0:T(1,128)} %broadcast_in_dim.6), calls=%async_computation | async-start | bytes 32768 | tf_op jit(solution)/shard_map/all_to_all | solution.py:9
  26.9 8.0 %all-to-all-done = f32[16,1,256]{2,1,0:T(1,128)S(1)} async-done(((f32[16,1,256]{2,1,0:T(1,128)}), f32[16,1,256]{2,1,0:T(1,128)S(1)}, u32[]{:S(2)}, u32[]{:S(2)}) %all-to-all-start) | async-done | bytes 16416 | tf_op jit(solution)/shard_map/all_to_all | solution.py:9
  35.0 0.1 dynamic_slice.6
  35.1 67.9 %reduce-scatter.2.cloned.1.call-done = f32[16,2688]{1,0:T(8,128)} async-done(((f32[256,2688]{1,0:T(8,128)}), f32[16,2688]{1,0:T(8,128)}) %reduce-scatter.2.cloned.1.call-update) | async-done | bytes 172048 | tf_op jit(solution)/shard_map/reduce_scatter | solution.py:23
  103.0 1.0 fusion.22
  104.0 47.6 %all_gather.3 = bf16[256,1792]{1,0:T(8,128)(2,1)S(1)} all-gather(bf16[16,1792]{1,0:T(8,128)(2,1)S(1)} %pad_maximum_fusion.2), channel_id=1, replica_groups=mesh['tp'=16,'lat'=32] {'tp'}, dimensions={0}, use_global_device_ids=true | all-gather | bytes 974848 | tf_op jit(solution)/shard_map/all_gather | solution.py:30
  151.5 0.5 fusion.9
  152.0 0.0 copy-done.2
  152.0 0.0 copy-start.7
  152.0 0.0 copy-start.6
  152.0 0.5 fusion
  152.5 38.4 %all_to_all.27 = f32[32,8,512]{2,1,0:T(8,128)S(1)} all-to-all(f32[32,8,512]{2,1,0:T(8,128)S(1)} %fusion), channel_id=1, replica_groups=mesh['tp'=16,'lat'=32] {'lat'}, dimensions={0} | all-to-all | bytes 1048576 | tf_op jit(solution)/shard_map/all_to_all | solution.py:41
  191.0 0.1 broadcast_in_dim.7
  191.0 22.5 %all_to_all.28 = f32[32,8,512]{2,1,0:T(8,128)S(1)} all-to-all(f32[32,8,512]{2,1,0:T(8,128)S(1)} %broadcast_in_dim.7), channel_id=1, replica_groups=mesh['tp'=16,'lat'=32] {'lat'}, dimensions={0} | all-to-all | bytes 1048576 | tf_op jit(solution)/shard_map/all_to_all | solution.py:9
  213.5 0.0 copy-done.7
  213.5 0.1 fusion.3
  213.6 0.6 broadcast_in_dim.8
  214.3 22.4 %all-to-all-start.3 = ((f32[16,1,256]{2,1,0:T(1,128)}), f32[16,1,256]{2,1,0:T(1,128)S(1)}, u32[]{:S(2)}, u32[]{:S(2)}) async-start(f32[16,1,256]{2,1,0:T(1,128)} %broadcast_in_dim.8), calls=%async_computation.4 | async-start | bytes 32768 | tf_op jit(solution)/shard_map/all_to_all | solution.py:9
  236.6 0.4 fusion.13
  237.0 7.7 %all-to-all-done.3 = f32[16,1,256]{2,1,0:T(1,128)S(1)} async-done(((f32[16,1,256]{2,1,0:T(1,128)}), f32[16,1,256]{2,1,0:T(1,128)S(1)}, u32[]{:S(2)}, u32[]{:S(2)}) %all-to-all-start.3) | async-done | bytes 16416 | tf_op jit(solution)/shard_map/all_to_all | solution.py:9
  244.7 0.2 fusion.6
  244.9 0.0 copy-start.3
  244.9 1.6 fusion.11
  246.5 0.1 pad_maximum_fusion.1
  246.6 0.0 copy-start.8
  246.6 0.0 copy-start.10
  246.6 0.0 copy-start.9
  246.7 1.2 copy.26
  247.9 0.0 copy-done.3
  247.9 6.0 %all-to-all-start.4 = ((f32[16,16,5,2,128]{4,1,2,3,0:T(8,128)}), f32[16,16,5,2,128]{4,1,2,3,0:T(8,128)S(1)}, u32[]{:S(2)}, u32[]{:S(2)}) async-start(f32[16,16,5,2,128]{4,1,2,3,0:T(8,128)} %copy.26), calls=%async_computation.5 | async-start | bytes 2621440 | tf_op jit(solution)/shard_map/all_to_all | solution.py:41
  253.9 0.1 constant_dynamic-slice_fusion
  254.0 0.1 copy.25
  254.7 0.3 compare_reduce_fusion
  255.0 0.1 and_convert_fusion
  255.1 58.4 %all-to-all-done.4 = f32[16,16,5,2,128]{4,1,2,3,0:T(8,128)S(1)} async-done(((f32[16,16,5,2,128]{4,1,2,3,0:T(8,128)}), f32[16,16,5,2,128]{4,1,2,3,0:T(8,128)S(1)}, u32[]{:S(2)}, u32[]{:S(2)}) %all-to-all-start.4) | async-done | bytes 1310752 | tf_op jit(solution)/shard_map/all_to_all | solution.py:41
  313.5 0.1 reduce_sum.59
  313.6 0.7 fusion.23
  (17 shorter events, 0.2 us)
Async XLA Ops:
  7.2 1.9 copy-start
  7.2 3.3 %copy-start.4 = (bf16[256,512]{1,0:T(8,128)(2,1)S(1)}, bf16[256,512]{1,0:T(8,128)(2,1)}, u32[]{:S(2)}) copy-start(bf16[256,512]{1,0:T(8,128)(2,1)} %param.17) | copy-start | bytes 786436
  7.2 3.3 %copy-start.5 = (bf16[896,512]{1,0:T(8,128)(2,1)S(1)}, bf16[896,512]{1,0:T(8,128)(2,1)}, u32[]{:S(2)}) copy-start(bf16[896,512]{1,0:T(8,128)(2,1)} %param.16) | copy-start | bytes 2752516
  7.2 95.8 %reduce-scatter.2.cloned.1.call-start = ((), (), s32[]{:S(2)}) async-start(), calls=%async_computation.6 | async-start | bytes 2924544 | tf_op jit(solution)/shard_map/reduce_scatter | solution.py:23
  12.7 0.9 copy-start.1
  12.7 139.3 %copy-start.2 = (bf16[512,896]{1,0:T(8,128)(2,1)S(1)}, bf16[512,896]{1,0:T(8,128)(2,1)}, u32[]{:S(2)}) copy-start(bf16[512,896]{1,0:T(8,128)(2,1)} %param.15) | copy-start | bytes 2752516
  14.4 20.5 %all-to-all-start = ((f32[16,1,256]{2,1,0:T(1,128)}), f32[16,1,256]{2,1,0:T(1,128)S(1)}, u32[]{:S(2)}, u32[]{:S(2)}) async-start(f32[16,1,256]{2,1,0:T(1,128)} %broadcast_in_dim.6), calls=%async_computation | async-start | bytes 32768 | tf_op jit(solution)/shard_map/all_to_all | solution.py:9
  152.0 61.5 %copy-start.7 = (f32[512]{0:T(512)S(1)}, f32[512]{0:T(512)}, u32[]{:S(2)}) copy-start(f32[512]{0:T(512)} %param.13) | copy-start | bytes 6148
  152.0 84.6 %copy-start.6 = (bf16[5,512,128]{2,1,0:T(8,128)(2,1)S(1)}, bf16[5,512,128]{2,1,0:T(8,128)(2,1)}, u32[]{:S(2)}) copy-start(bf16[5,512,128]{2,1,0:T(8,128)(2,1)} %param.18) | copy-start | bytes 1966084
  214.3 30.4 %all-to-all-start.3 = ((f32[16,1,256]{2,1,0:T(1,128)}), f32[16,1,256]{2,1,0:T(1,128)S(1)}, u32[]{:S(2)}, u32[]{:S(2)}) async-start(f32[16,1,256]{2,1,0:T(1,128)} %broadcast_in_dim.8), calls=%async_computation.4 | async-start | bytes 32768 | tf_op jit(solution)/shard_map/all_to_all | solution.py:9
  244.9 3.0 copy-start.3
  246.6 7.3 %copy-start.8 = (s32[256,64]{0,1:T(8,128)S(1)}, s32[256,64]{0,1:T(8,128)}, u32[]{:S(2)}) copy-start(s32[256,64]{0,1:T(8,128)} %param.23) | copy-start | bytes 196612
  246.6 8.1 %copy-start.10 = (s32[5]{0:T(128)S(1)}, s32[5]{0:T(128)}, u32[]{:S(2)}) copy-start(s32[5]{0:T(128)} %param.21) | copy-start | bytes 64
  246.6 66.9 %copy-start.9 = (f32[5,128]{1,0:T(8,128)S(1)}, f32[5,128]{1,0:T(8,128)}, u32[]{:S(2)}) copy-start(f32[5,128]{1,0:T(8,128)} %param.19) | copy-start | bytes 7684
  247.9 65.6 %all-to-all-start.4 = ((f32[16,16,5,2,128]{4,1,2,3,0:T(8,128)}), f32[16,16,5,2,128]{4,1,2,3,0:T(8,128)S(1)}, u32[]{:S(2)}, u32[]{:S(2)}) async-start(f32[16,16,5,2,128]{4,1,2,3,0:T(8,128)} %copy.26), calls=%async_computation.5 | async-start | bytes 2621440 | tf_op jit(solution)/shard_map/all_to_all | solution.py:41
Sparse Core Ops, SparseCore 0:
  12.9 90.0 reduce-scatter.1
where the time goes:
time: 322 us; the launch traced here: 321 us
  waiting for transfers between devices  142 us (44%)
  blocking collectives  108 us (34%)
  starting transfers between devices  40.9 us (13%)
  between operations  14.9 us (5%)
  matrix products  6.57 us (2%)
  other arithmetic  4.55 us (1%)
  local copies, waits for them, and re-layouts  3.73 us (1%)
    reduce_scatter x1, waiting for transfers between devices, in_one_piece(): lax.psum_scatter(both, axis, scatter_dimension=dim, tiled=True)  67.9 us
    all_to_all x1, waiting for transfers between devices, sum_at_owner(): pieces = lax.all_to_all(in_blocks(x, dim, devices), axis, 0, 0, tiled=True)  58.4 us
    all_gather x1, blocking collectives, in_one_piece_2(): result = lax.all_gather(both, axis, axis=dim, tiled=True)  47.6 us
    all_to_all x1, blocking collectives, sum_at_owner(): pieces = lax.all_to_all(in_blocks(x, dim, devices), axis, 0, 0, tiled=True)  38.4 us
    all_to_all x2, starting transfers between devices, copy_for_each(): lax.all_to_all(jnp.broadcast_to(x[None], (devices, *x.shape)), axis, 0, 0...  34.8 us
    all_to_all x1, blocking collectives, copy_for_each(): lax.all_to_all(jnp.broadcast_to(x[None], (devices, *x.shape)), axis, 0, 0...  22.5 us
    all_to_all x2, waiting for transfers between devices, copy_for_each(): lax.all_to_all(jnp.broadcast_to(x[None], (devices, *x.shape)), axis, 0, 0...  15.7 us
  transfers between devices with their start and end apart: 4, of which 4 were waited for; matrix products, arithmetic and copies ran while one was open for 1% of the time, Pallas kernels for 0%

commit v1 on v0

v1 whole, which is shorter than its diff:
```python
import jax
import jax.numpy as jnp
from jax import lax
from jax.experimental import pallas as pl
from jax.experimental.pallas import tpu as pltpu
from jax.sharding import PartitionSpec as P

BF = jnp.bfloat16
F32 = jnp.float32
WIDTH = 8192
TOK = 256
G = 7
NR = 2
RT, CT = 256 // NR, 128 // NR
HT = CT // 2
NS = G * NR
PART = NS // 2
FINISH = 3 * NR // 2
GATHER = 5 * NR
SKIP = NS - 3 * NR // 2
STEPS = 2 * NS + 2
VMEM = pl.BlockSpec(memory_space=pltpu.VMEM)
SMEM = pl.BlockSpec(memory_space=pltpu.SMEM)
HBM = pl.BlockSpec(memory_space=pltpu.HBM)


def dot(a, b):
    return jnp.dot(a, b, preferred_element_type=F32)


def dot_t(a, b, precision=None):
    return lax.dot_general(
        a, b, (((1,), (1,)), ((), ())), precision=precision, preferred_element_type=F32
    )


def row_sums(x):
    folded = x[:, 0:128]
    for k in range(1, x.shape[1] // 128):
        folded = folded + x[:, 128 * k : 128 * (k + 1)]
    return dot_t(jnp.ones((8, 128), F32), folded, lax.Precision.HIGHEST)


def as_column(row, n):
    full = jnp.broadcast_to(row, (n, n))
    same = lax.broadcasted_iota(jnp.int32, (n, n), 0) == lax.broadcasted_iota(jnp.int32, (n, n), 1)
    return jnp.sum(jnp.where(same, full, 0.0), axis=1, keepdims=True)


def copy(src, dst, send_sem, recv_sem, **device):
    return pltpu.make_async_remote_copy(
        src_ref=src,
        dst_ref=dst,
        send_sem=send_sem,
        recv_sem=recv_sem,
        device_id=device,
        device_id_type=pl.DeviceIdType.MESH,
    )


def loop(n, body, start=0):
    def step(i, carry):
        body(i)
        return carry

    lax.fori_loop(start, n, step, 0)


def kernel(
    resid_h,
    gain_h,
    w_gate_h,
    w_up_h,
    w_down_h,
    cot_h,
    enc_h,
    bias_h,
    dec_h,
    tile_blocks_h,
    owner_counts,
    tokens_h,
    rg_out,
    att_out,
    resid,
    gain,
    w_gate,
    w_up,
    w_down,
    cot,
    enc,
    bias,
    dec,
    tile_blocks,
    tokens,
    part,
    scaled,
    psend,
    precv,
    rs_recv,
    rs_send,
    x_recv,
    d_all,
    acc,
    rinv_s,
    sq_own,
    sq_recv,
    fsend,
    frecv,
    hsend,
    hrecv,
    n_own,
    n_recv,
    rg_own,
    rg_all,
    terms,
    tp_send,
    tp_recv,
    tz_send,
    tz_recv,
    gate_term,
    psem,
    precvsem,
    rssem,
    rsrecv,
    xsem,
    agsend,
    agrecv,
    agother,
    sqsem,
    fsem,
    hsem,
    nsem,
    rgsem,
    tpsem,
    tzsem,
    insem,
):
    t, l = lax.axis_index("tp"), lax.axis_index("lat")
    z, c = lax.div(t, 2), lax.rem(t, 2)
    p, h = lax.div(l, 2), lax.rem(l, 2)
    y, x = lax.div(p, 4), lax.rem(p, 4)
    other = t + 1 - 2 * c
    right = lax.div(z, 4)
    step_in = 1 - 2 * right
    q = z + right * (7 - 2 * z)
    inward = t + 2 * step_in
    outward = t - 2 * step_in
    middle = lax.div(q, 3)
    beside = lax.div(q, 2) - middle
    lag = NS + (GATHER - NS) * beside + (FINISH + 1 - NS) * middle
    mate = l + 1 - 2 * h
    u = h * 16 + t

    ahead = 2 + (NS - 2) // 3 * q
    early = lax.div(q + 2, 3)
    flag = lag + 1 + early
    group = 8 * lax.rem(x + y, 2) + lax.div(p, 2)

    def owner_of(g):
        e = lax.rem(g, 8)
        return 2 * e + lax.rem(lax.div(g, 8) + lax.div(e, 2), 2)

    def group_of(pp):
        return 8 * lax.rem(lax.rem(pp, 4) + lax.div(pp, 4), 2) + lax.div(pp, 2)

    def peer_xy(j):
        return lax.rem(y + lax.div(j, 4), 4) * 4 + lax.rem(x + lax.rem(j, 4), 4)

    def peer_tp(j):
        return lax.rem(t + j, 16)

    def peer_z(j):
        return lax.rem(z + j, 8)

    loads = [
        pltpu.make_async_copy(src, dst, insem.at[k])
        for k, (src, dst) in enumerate(
            (
                (resid_h, resid),
                (gain_h, gain),
                (w_gate_h.at[:, 0:256], w_gate.at[:, 0:256]),
                (w_up_h.at[:, 0:256], w_up.at[:, 0:256]),
                (cot_h, cot),
                (w_down_h.at[0:256], w_down.at[0:256]),
                (w_gate_h.at[:, 256:896], w_gate.at[:, 256:896]),
                (w_up_h.at[:, 256:896], w_up.at[:, 256:896]),
                (w_down_h.at[256:896], w_down.at[256:896]),
                (enc_h, enc),
                (tokens_h, tokens),
                (dec_h, dec),
                (bias_h, bias),
                (tile_blocks_h, tile_blocks),
            )
        )
    ]
    for load in loads[:9]:
        load.start()

    barrier = pltpu.get_barrier_semaphore()

    def greet(**device):
        pl.semaphore_signal(
            barrier, inc=1, device_id=device, device_id_type=pl.DeviceIdType.MESH
        )

    loop(16, lambda j: greet(tp=j, lat=mate))
    loop(16, lambda j: greet(tp=peer_tp(j), lat=l), 1)
    loop(16, lambda j: greet(tp=t, lat=peer_xy(j) * 2 + h), 1)

    loads[0].wait()
    loads[1].wait()
    resid_f = resid[...].astype(F32)
    scaled[...] = (resid_f * gain[...]).astype(BF)
    sq_own[...] = row_sums(resid_f * resid_f)[0:1]
    sq_recv[pl.ds(t, 1)] = sq_own[...][None]

    def products(n):
        g = lax.rem(n, G)
        lanes = pl.ds(pl.multiple_of(g * 128, 128), 128)
        rows = pl.ds(pl.multiple_of(lax.div(n, G) * RT, RT), RT)
        part[n, :, 0:128] = dot(scaled[rows, :], w_gate[:, lanes])
        part[n, :, 128:256] = dot(scaled[rows, :], w_up[:, lanes])
        part[n, :, 256:384] = dot_t(cot[rows, :], w_down[lanes, :])
        psend[n] = part[n, pl.ds(pl.multiple_of((1 - c) * CT, CT), CT), :].astype(BF)

    def to_partner(g):
        return copy(psend.at[g], precv.at[g], psem, precvsem.at[g], tp=other)

    for load in loads[2:6]:
        load.wait()
    products(0)

    @pl.when(q == 0)
    def _():
        rs_recv[...] = jnp.zeros_like(rs_recv)

    for load in loads[9:]:
        load.start()

    pl.semaphore_wait(barrier, 46)

    to_partner(0).start()

    def all_of(ref, send_sem, recv_sem):
        return copy(ref, ref, send_sem, recv_sem, tp=other)

    def squares_to(j):
        return copy(sq_own, sq_recv.at[t], sqsem.at[0], sqsem.at[1], tp=peer_tp(j))

    squares = all_of(sq_recv.at[0:15], sqsem.at[0], sqsem.at[1])

    loop(16, lambda j: squares_to(j).start(), 1)

    def first(g):
        products(g)
        to_partner(g).start()

    for load in loads[6:9]:
        load.wait()
    loop(ahead, first, 1)
    acc[...] = jnp.zeros_like(acc)

    def in_rs(k, g):
        return copy(rs_send.at[g, k], rs_recv.at[g, k], rssem, rsrecv.at[k, g], tp=inward)

    def across(k, g):
        return copy(rs_send.at[g, k], x_recv.at[g, k], rssem, xsem.at[k, g], tp=inward)

    def half_rows(k):
        return pl.ds(pl.multiple_of(c * CT + k * HT, HT), HT)

    def scatter_step(g):
        to_partner(g).wait_recv()
        for k in range(2):

            @pl.when(q > 0)
            def _():
                in_rs(k, g).wait_recv()

            value = part[g, half_rows(k), :] + precv[g, k * HT : (k + 1) * HT, :].astype(F32)
            value = value + rs_recv[g, k].astype(F32)
            rs_send[g, k] = value.astype(BF)

            @pl.when(q < 3)
            def _():
                in_rs(k, g).start()

            @pl.when(q == 3)
            def _():
                across(k, g).start()
                part[g, half_rows(k), :] = value

    def ag(where, k, g, **device):
        at = d_all.at[g, c, k]
        return copy(at, at, agsend.at[where], agrecv.at[k, g], **device)

    def to_other(g):
        at = d_all.at[g, c]
        return copy(at, at, agsend.at[2], agother.at[g], tp=other)

    def finish_step(g):
        for k in range(2):
            across(k, g).wait_recv()
            value = part[g, half_rows(k), :] + x_recv[g, k].astype(F32)
            first_row = lax.div(g, G) * RT + c * CT + k * HT
            scale = rinv_s[pl.ds(pl.multiple_of(first_row, HT), HT), :]
            gate, up = scale * value[:, 0:128], scale * value[:, 128:256]
            hgrad = value[:, 256:384]
            sig = jax.nn.sigmoid(gate)
            d_all[g, c, k, :, 0:128] = (
                hgrad * up * sig * (1.0 + gate * (1.0 - sig))
            ).astype(BF)
            d_all[g, c, k, :, 128:256] = (hgrad * gate * sig).astype(BF)
            ag(0, k, g, tp=outward).start()

            @pl.when(g >= SKIP)
            def _():
                ag(1, k, g, tp=outward - 2 * step_in).start()

        to_other(g).start()

    def passes(g):
        return (q > 0) & ((q != 2) | (g < SKIP))

    def gather_step(g):
        for k in range(2):
            ag(0, k, g, tp=outward).wait_recv()

            @pl.when(passes(g))
            def _():
                ag(0, k, g, tp=outward).start()

        to_other(g).start()

    def feature_step(n):
        to_other(n).wait_recv()
        g = lax.rem(n, G)
        lanes = pl.ds(pl.multiple_of(g * 128, 128), 128)
        rows = pl.ds(pl.multiple_of(lax.div(n, G) * RT, RT), RT)
        d = d_all[n].reshape(RT, 256)
        acc[rows, :] += dot_t(d[:, 0:128], w_gate[:, lanes]) + dot_t(d[:, 128:256], w_up[:, lanes])

    def feat_to(k, into):
        return copy(fsend.at[k], frecv.at[p], fsem.at[0], fsem.at[1], lat=into * 2 + h)

    feats = all_of(frecv.at[0:15], fsem.at[0], fsem.at[1])

    def feat_start(half):
        k0 = half * 8
        rows = pl.ds(pl.multiple_of(half * 128, 128), 128)
        fsend[pl.ds(k0, 8)] = acc[rows, :].astype(BF).reshape(8, 16, 512)

        def send(e):
            k = k0 + lax.rem(lax.div(p, 2) + e, 8)
            into = owner_of(k)

            @pl.when(into != p)
            def _():
                feat_to(k, into).start()

        loop(8, send)

    def inverse_norms():
        squares.wait_recv()
        total = sq_recv[0]
        for k in range(1, 16):
            total = total + sq_recv[k]
        column = as_column(lax.rsqrt(total / WIDTH + 1e-05), TOK)
        rinv_s[...] = jnp.broadcast_to(column, (TOK, 128))

    def tiles_to_partner(kind):
        return copy(
            tp_send.at[kind], tp_recv.at[kind], tpsem.at[0, kind], tpsem.at[1, kind], tp=other
        )

    def tiles_to(kind, j):
        zz = peer_z(j)
        return copy(
            tz_send.at[kind, zz],
            tz_recv.at[kind, z],
            tzsem.at[kind, 0],
            tzsem.at[kind, 1],
            tp=2 * zz + c,
        )

    def tiles_all(kind):
        return all_of(tz_recv.at[kind, 0:7], tzsem.at[kind, 0], tzsem.at[kind, 1])

    def tiles_start(kind):
        tp_send[kind] = terms[kind, :, 1 - c].astype(BF)
        tiles_to_partner(kind).start()

    def tiles_spread(kind):
        tiles_to_partner(kind).wait_recv()
        chip = terms[kind, :, c] + tp_recv[kind].astype(F32)
        terms[kind, :, c] = chip
        tz_send[kind] = chip.astype(BF)
        tz_recv[kind, z] = jnp.zeros((16, 640), BF)
        loop(8, lambda j: tiles_to(kind, j).start(), 1)

    def tiles_total(kind):
        tiles_all(kind).wait_recv()
        total = terms[kind, z, c]
        for k in range(8):
            total = total + tz_recv[kind, k].astype(F32)
        return total

    def pre_products():
        for load in loads[9:]:
            load.wait()
        for j in range(5):
            terms[0, :, :, :, 128 * j : 128 * (j + 1)] = dot(resid[...], enc[j]).reshape(
                8, 2, 16, 128
            )
        tiles_start(0)

    def step(s):
        @pl.when(s == NS * (1 - early))
        def _():
            pre_products()

        @pl.when(s < NS)
        def _():
            scatter_step(s)

        @pl.when(s + ahead < NS)
        def _():
            first(s + ahead)

        @pl.when(s == NS + (FINISH - NS) * early)
        def _():
            inverse_norms()

        @pl.when((q == 3) & (s >= FINISH) & (s < FINISH + NS))
        def _():
            finish_step(s - FINISH)

        @pl.when((s >= flag) & (s < flag + NS))
        def _():
            feature_step(s - flag)

            @pl.when(lax.rem(s - flag + 1, PART) == 0)
            def _():
                feat_start(lax.div(s - flag + 1, PART) - 1)

        @pl.when((q < 3) & (s >= lag) & (s < lag + NS))
        def _():
            gather_step(s - lag)

    loop(STEPS, step)

    frecv[p] = jnp.zeros((16, 512), BF)
    feats.wait_recv()
    own_rows = pl.ds(pl.multiple_of(group * 16, 16), 16)
    total = acc[own_rows, :]
    for k in range(16):
        total = total + frecv[k].astype(F32)
    hsend[...] = total.astype(BF)

    def to_mate():
        return copy(hsend, hrecv, hsem.at[0], hsem.at[1], lat=mate)

    to_mate().start()
    half = hsend[...].astype(F32)
    own_resid = resid[own_rows, :].astype(F32)
    n_own[...] = jnp.zeros_like(n_own)
    n_own[0:1, 0:16] = row_sums(own_resid * gain[...] * half)[0:1]
    n_recv[pl.ds(u, 1)] = n_own[...][None]

    def norm_to(j, half):
        return copy(
            n_own, n_recv.at[u], nsem.at[0], nsem.at[1], tp=peer_tp(j), lat=half
        )

    norms = all_of(n_recv.at[0:31], nsem.at[0], nsem.at[1])
    loop(16, lambda j: norm_to(j, mate).start())
    loop(16, lambda j: norm_to(j, l).start(), 1)

    lists = tokens[...]
    own_token = lax.broadcasted_iota(jnp.int32, (16, TOK), 0) + t * 16
    own_token = own_token == lax.broadcasted_iota(jnp.int32, (16, TOK), 1)
    for j in range(5):
        hits = jnp.max((lists == tile_blocks[j]).astype(F32), axis=0, keepdims=True)
        hits = jnp.broadcast_to(hits, (16, TOK))
        hit = jnp.sum(jnp.where(own_token, hits, 0.0), axis=1, keepdims=True)
        live = hit * jnp.where(owner_counts[0] > j, 1.0, 0.0)
        gate_term[:, 128 * j : 128 * (j + 1)] = jnp.broadcast_to(live, (16, 128))

    norms.wait_recv()
    norm = n_recv[0]
    for k in range(1, 32):
        norm = norm + n_recv[k]
    norm = as_column(norm[:, 0:16], 16)
    to_mate().wait_recv()
    feat = half + hrecv[...].astype(F32)
    rinv = rinv_s[own_rows, 0:1]
    rg_own[...] = (
        cot[own_rows, :].astype(F32)
        + rinv * gain[...] * feat
        - own_resid * (rinv * rinv * rinv * norm / WIDTH)
    ).astype(BF)

    def grad_to(j):
        pp = peer_xy(j)
        return copy(rg_own, rg_all.at[group], rgsem.at[0], rgsem.at[1], lat=pp * 2 + h)

    spread = all_of(rg_all.at[0:15], rgsem.at[0], rgsem.at[1])
    loop(16, lambda j: grad_to(j).start(), 1)
    tiles_spread(0)
    rg_all[group] = rg_own[...]
    spread.wait_recv()
    grads = rg_all[...].reshape(TOK, 512)
    for j in range(5):
        terms[1, :, :, :, 128 * j : 128 * (j + 1)] = dot_t(grads, dec[j]).reshape(8, 2, 16, 128)
    tiles_start(1)
    rg_out[...] = grads
    tiles_spread(1)
    pre = tiles_total(0)
    for j in range(5):
        lanes = slice(128 * j, 128 * (j + 1))
        gate_term[:, lanes] *= -jnp.maximum(pre[:, lanes] + bias[j : j + 1, :], 0.0)

    all_of(psend, psem, precvsem.at[0]).wait_send()
    all_of(rs_send, rssem, rsrecv.at[0, 0]).wait_send()

    def blocks_sent(where, n):
        all_of(d_all.at[0:n, 0], agsend.at[where], agrecv.at[0, 0]).wait_send()

    @pl.when(lax.rem(q, 2) == 1)
    def _():
        blocks_sent(0, NS)

    @pl.when(q == 2)
    def _():
        blocks_sent(0, SKIP)

    @pl.when(q == 3)
    def _():
        blocks_sent(1, NS - SKIP)

    blocks_sent(2, NS)
    squares.wait_send()
    feats.wait_send()
    spread.wait_send()
    to_mate().wait_send()
    norms.wait_send()
    for kind in range(2):
        tiles_to_partner(kind).wait_send()
    tiles_all(0).wait_send()

    grad = tiles_total(1)
    for j in range(5):
        lanes = slice(128 * j, 128 * (j + 1))
        att_out[j] = gate_term[:, lanes] * grad[:, lanes]

    tiles_all(1).wait_send()


def in_hbm(x):
    return pltpu.with_memory_space_constraint(x, pltpu.HBM)


def on_device(
    resid,
    gain,
    w_gate,
    w_up,
    w_down,
    cotangent,
    enc_tiles,
    enc_bias,
    dec_tiles,
    tile_blocks,
    owner_counts,
    token_blocks,
):
    dma = pltpu.SemaphoreType.DMA
    vmem = pltpu.VMEM
    resid_grad, attribution = pl.pallas_call(
        kernel,
        out_shape=(
            jax.ShapeDtypeStruct((TOK, 512), BF),
            jax.ShapeDtypeStruct((5, 16, 128), F32),
        ),
        in_specs=[HBM] * 10 + [SMEM, HBM],
        out_specs=(VMEM, VMEM),
        scratch_shapes=[
            vmem((TOK, 512), BF),
            vmem((1, 512), F32),
            vmem((512, 896), BF),
            vmem((512, 896), BF),
            vmem((896, 512), BF),
            vmem((TOK, 512), BF),
            vmem((5, 512, 128), BF),
            vmem((5, 128), F32),
            vmem((5, 128, 512), BF),
            pltpu.SMEM((5,), jnp.int32),
            vmem((64, TOK), jnp.int32),
            vmem((NS, RT, 384), F32),
            vmem((TOK, 512), BF),
            vmem((NS, CT, 384), BF),
            vmem((NS, CT, 384), BF),
            vmem((NS, 2, HT, 384), BF),
            vmem((NS, 2, HT, 384), BF),
            vmem((NS, 2, HT, 384), BF),
            vmem((NS, 2, 2, HT, 256), BF),
            vmem((TOK, 512), F32),
            vmem((TOK, 128), F32),
            vmem((1, TOK), F32),
            vmem((16, 1, TOK), F32),
            vmem((16, 16, 512), BF),
            vmem((16, 16, 512), BF),
            vmem((16, 512), BF),
            vmem((16, 512), BF),
            vmem((1, 128), F32),
            vmem((32, 1, 128), F32),
            vmem((16, 512), BF),
            vmem((16, 16, 512), BF),
            vmem((2, 8, 2, 16, 640), F32),
            vmem((2, 8, 16, 640), BF),
            vmem((2, 8, 16, 640), BF),
            vmem((2, 8, 16, 640), BF),
            vmem((2, 8, 16, 640), BF),
            vmem((16, 640), F32),
            dma(()),
            dma((NS,)),
            dma(()),
            dma((2, NS)),
            dma((2, NS)),
            dma((3,)),
            dma((2, NS)),
            dma((NS,)),
            dma((2,)),
            dma((2,)),
            dma((2,)),
            dma((2,)),
            dma((2,)),
            dma((2, 2)),
            dma((2, 2)),
            dma((14,)),
        ],
        compiler_params=pltpu.CompilerParams(
            collective_id=0, has_side_effects=True, vmem_limit_bytes=48 * 1000 * 1000
        ),
    )(
        *map(
            in_hbm,
            (
                resid,
                gain.reshape(1, 512),
                w_gate,
                w_up,
                w_down,
                cotangent,
                enc_tiles,
                enc_bias,
                dec_tiles,
                tile_blocks,
            ),
        ),
        owner_counts,
        in_hbm(token_blocks.T),
    )
    return resid_grad, attribution.transpose(1, 0, 2)


def solution(mesh):
    placed = (
        P(None, "tp"),
        P("tp"),
        P("tp", "lat"),
        P("tp", "lat"),
        P("lat", "tp"),
        P(None, "tp"),
        P("lat", "tp", None),
        P("lat", None),
        P("lat", None, "tp"),
        P("lat"),
        P("lat"),
        P(),
    )
    return jax.shard_map(
        on_device,
        mesh=mesh,
        in_specs=placed,
        out_specs=(P(None, "tp"), P("tp", "lat", None)),
        check_vma=False,
    )
```

time: 322 us -> 88.5 us (0.27)
  the two profiles are of different devices: /device:TPU:65 before, /device:TPU:33 now
where the time goes in v1:
time: 88.5 us; the launch traced here: 88.3 us
  Pallas kernels  85.7 us (97%)
  local copies, waits for them, and re-layouts  1.32 us (1%)
  between operations  1.29 us (1%)
    pallas_call x1, Pallas kernels, on_device(): pl.pallas_call(kernel, out_shape=(jax.ShapeDtypeStruct((TOK, 512), BF), j...  85.7 us

profile of v1, /device:TPU:33, one launch (start us, length us, event | category | flops | bytes accessed | tf_op | source)
XLA Modules:
  0.0 88.3 jit_solution(3597299513462918737)
XLA Ops:
  1.3 85.7 %shard_map.131 = (bf16[256,512]{1,0:T(8,128)(2,1)S(1)}, f32[5,16,128]{2,1,0:T(8,128)S(1)}) custom-call(bf16[256,512]{1,0:T(8,128)(2,1)} %resid_h.1, f32[1,512]{1,0:T(1,128)} %bitcast.5, bf16[512,896]{1,0:T(8,128)(2,1)} %w_gate_h.1, bf16[512,896]{1,0:T(8,128)(2,1)} %w_up_h.1, bf16[896,512]{1,0:T(8,128)(2,1)} %w_down_h.1, bf16[256,512]{1,0:T(8,128)(2,1)} %cot_h.1, ...), custom_call_target="tpu_custom_call" | custom-call | tf_op jit(solution)/shard_map/pallas_call | solution.py:579
  87.0 0.7 copy.17
  87.7 0.6 copy.18
